TPU v7x, 512 devices: a whole 4x8x8 slice. The times are simulated.
512 devices in a mesh: dp: 64 (over x, y, core), code: 8 (over z).
Axes of the slice: x: 4, y: 8, z: 8, core: 2. Of those that a mesh axis runs over, the one named last changes fastest.
Arguments:
- items: float32 [65536, 512], P(('dp', 'code')), may hold values from -6 to 6
- codewords: float32 [8192, 512], P('code'), may hold values from -6 to 6
- assign: int32 [65536], P('dp'), may hold values from 0 to 8191, as said below
Outputs:
- new_codewords: float32 [8192, 512], P('code', 'dp')
- residual: float32 [65536, 512], P(('dp', 'code'))
Inputs may be any that keep to these rules, and one draw needn't show every extreme that they name: `assign`: the items are laid out in aligned blocks of 128 (the items of one device). Splitting the codewords into equal ranges, one per index of code, the items of one block name codewords of exactly half of the ranges, 32 items for each such range.
All inputs are finite; a program needn't handle non-finite values.
Results may differ from a plain program's by a relative error of at most 0.0003.
Values sent between devices are 32-bit elements; how exact they have to be, the bound alone decides.
No kernel may reach another device: no remote copies, remote signals or barrier semaphores. Data moves between devices by JAX's collectives and lax.ppermute only.
A program may use at most 64 MiB of HBM per device.

v0:
```python
import jax
import jax.numpy as jnp
from jax import lax
from jax.sharding import PartitionSpec as P

K = 8192
ITERS = 3
epsilon = 1e-05
inverse_temp = 64.0


def unit_rows(values):
    return values * lax.rsqrt(jnp.mean(values * values, axis=-1, keepdims=True) + epsilon)


def kernel_of(rows_block, scaled):
    return jnp.exp(
        jnp.dot(
            unit_rows(rows_block),
            scaled.T,
            precision=lax.Precision.HIGHEST,
            preferred_element_type=jnp.float32,
        )
    )


def column_scale(col_part):
    summed = lax.psum(col_part, "dp")
    return 1.0 / (K * summed)


def row_scaling(row_part, total_items):
    summed = lax.psum(row_part, "code")
    return 1.0 / (total_items * summed)


def body(items, codewords, assign):
    code_count = lax.axis_size("code")
    dp_count = lax.axis_size("dp")
    local_codes = codewords.shape[0]
    width = items.shape[1]
    own_rows = items.shape[0]
    total_items = own_rows * code_count * dp_count
    scaled = unit_rows(codewords) * (inverse_temp / width)
    gathered = lax.all_gather(items, "code", axis=0, tiled=True)
    kernel_vals = kernel_of(gathered, scaled)
    col_part = jnp.sum(kernel_vals, axis=0)
    row_scale = jnp.ones((kernel_vals.shape[0],), jnp.float32)
    for sweep_index in range(ITERS):
        col_scale = column_scale(col_part)
        row_part = jnp.dot(
            kernel_vals,
            col_scale,
            precision=lax.Precision.HIGHEST,
            preferred_element_type=jnp.float32,
        )
        row_scale = row_scaling(row_part, total_items)
        col_part = jnp.dot(
            row_scale,
            kernel_vals,
            precision=lax.Precision.HIGHEST,
            preferred_element_type=jnp.float32,
        )
    mass = lax.psum(col_part, "dp")
    numerator = lax.dot_general(
        kernel_vals,
        row_scale[:, None] * gathered,
        (((0,), (0,)), ((), ())),
        precision=lax.Precision.HIGHEST,
        preferred_element_type=jnp.float32,
    )
    owned_sums = lax.psum_scatter(numerator, "dp", scatter_dimension=1, tiled=True)
    new_codewords = owned_sums / mass[:, None]
    my_code = lax.axis_index("code")
    offset = my_code * local_codes
    index_rows = assign - offset
    inside = (index_rows >= 0) & (index_rows < local_codes)
    picked = jnp.take(codewords, jnp.clip(index_rows, 0, local_codes - 1), axis=0)
    looked = lax.psum_scatter(
        jnp.where(inside[:, None], picked, jnp.float32(0.0)),
        "code",
        scatter_dimension=0,
        tiled=True,
    )
    residual = items - looked
    return (new_codewords, residual)


def solution(mesh):
    in_specs = (P(("dp", "code"), None), P("code", None), P("dp"))
    out_specs = (P("code", "dp"), P(("dp", "code"), None))
    return jax.shard_map(body, mesh=mesh, in_specs=in_specs, out_specs=out_specs, check_vma=False)
```

profile of v0, /device:TPU:16, one launch (start us, length us, event | category | flops | bytes accessed | tf_op | source)
XLA Modules:
  0.0 675.3 jit_solution(14707872022729318664)
XLA Ops:
  7.2 0.0 all-gather.2.cloned.1.call-start
  7.2 0.7 all-gather.2.cloned.1.call-update
  7.9 0.0 reduce-scatter.5.cloned.1.call-start
  7.9 0.7 fusion.23
  8.6 0.0 copy-start.4
  8.6 5.6 gather_fusion
  14.3 0.0 copy-done.4
  14.3 2.0 select_select_fusion
  16.3 0.0 copy-start
  16.3 0.0 reduce-scatter.5.cloned.1.call-update
  16.3 0.0 reduce-scatter.3.cloned.1.call-start
  16.4 1.5 copy-done
  17.9 0.2 multiply_reduce_fusion
  18.1 41.1 %all-gather.2.cloned.1.call-done = f32[1024,512]{1,0:T(8,128)} async-done(((f32[128,512]{1,0:T(8,128)}), f32[1024,512]{1,0:T(8,128)}) %all-gather.2.cloned.1.call-update) | async-done | bytes 2097168 | tf_op jit(solution)/shard_map/all_gather | solution.py:45
  59.2 0.0 copy-start.1
  59.2 2.0 multiply_reduce_fusion.1
  61.2 0.3 copy-done.1
  61.5 9.1 %exponential_reduce_fusion = (f32[1024]{0:T(1024)S(1)}, f32[1024,1024]{1,0:T(8,128)}) fusion(f32[1024,512]{1,0:T(8,128)S(1)} %copy-done, f32[1024]{0:T(1024)S(1)} %add_rsqrt_fusion, f32[1024,512]{1,0:T(8,128)S(1)} %copy-done.1, f32[1024]{0:T(1024)S(1)} %add_rsqrt_fusion.1), kind=kOutput, calls=%fused_computation.15 | convolution fusion | flops 6445071360 | bytes 8400896 | tf_op jit(solution)/shard_map/dot_general | solution.py:18
  70.5 114.3 %psum.49 = f32[1024]{0:T(1024)S(1)} all-reduce(f32[1024]{0:T(1024)S(1)} %get-tuple-element.4), channel_id=1, replica_groups=mesh['dp'=64,'code'=8] {'dp'}, use_global_device_ids=true, to_apply=%region_3.0 | all-reduce | flops 1024 | bytes 8192 | tf_op jit(solution)/shard_map/psum | solution.py:28
  184.8 6.2 fusion.12
  191.0 16.1 %psum.50 = f32[1024]{0:T(1024)S(1)} all-reduce(f32[1024]{0:T(1024)S(1)} %bitcast.21), channel_id=1, replica_groups=mesh['dp'=64,'code'=8] {'code'}, use_global_device_ids=true, to_apply=%region_4.0 | all-reduce | flops 1024 | bytes 8192 | tf_op jit(solution)/shard_map/psum | solution.py:33
  207.1 4.5 fusion.10
  211.6 124.2 %psum.51 = f32[1024]{0:T(1024)S(1)} all-reduce(f32[1024]{0:T(1024)S(1)} %bitcast.23), channel_id=1, replica_groups=mesh['dp'=64,'code'=8] {'dp'}, use_global_device_ids=true, to_apply=%region_5.0 | all-reduce | flops 1024 | bytes 8192 | tf_op jit(solution)/shard_map/psum | solution.py:28
  335.8 6.2 fusion.8
  342.0 14.2 %psum.52 = f32[1024]{0:T(1024)S(1)} all-reduce(f32[1024]{0:T(1024)S(1)} %bitcast.25), channel_id=1, replica_groups=mesh['dp'=64,'code'=8] {'code'}, use_global_device_ids=true, to_apply=%region_6.0 | all-reduce | flops 1024 | bytes 8192 | tf_op jit(solution)/shard_map/psum | solution.py:33
  356.2 4.5 fusion.6
  360.7 124.0 %psum.53 = f32[1024]{0:T(1024)S(1)} all-reduce(f32[1024]{0:T(1024)S(1)} %bitcast.27), channel_id=1, replica_groups=mesh['dp'=64,'code'=8] {'dp'}, use_global_device_ids=true, to_apply=%region_7.0 | all-reduce | flops 1024 | bytes 8192 | tf_op jit(solution)/shard_map/psum | solution.py:28
  484.7 0.0 copy-start.2
  484.7 6.3 fusion.4
  491.1 16.4 %psum.54 = f32[1024]{0:T(1024)S(1)} all-reduce(f32[1024]{0:T(1024)S(1)} %bitcast.29), channel_id=1, replica_groups=mesh['dp'=64,'code'=8] {'code'}, use_global_device_ids=true, to_apply=%region_8.0 | all-reduce | flops 1024 | bytes 8192 | tf_op jit(solution)/shard_map/psum | solution.py:33
  507.4 0.0 copy-done.2
  507.5 10.3 %fusion.2 = f32[1024,512]{0,1:T(8,128)} fusion(f32[1024,1024]{1,0:T(8,128)} %get-tuple-element.5, f32[1024,512]{1,0:T(8,128)S(1)} %copy-done.2, f32[1024]{0:T(1024)S(1)} %multiply_divide_fusion), kind=kOutput, calls=%fused_computation.3 | convolution fusion | flops 6442975232 | bytes 8392704 | tf_op jit(solution)/shard_map/dot_general | solution.py:65
  517.8 0.0 reduce-scatter.3.cloned.1.call-update
  517.8 0.0 copy-start.3
  517.8 4.5 fusion
  522.4 124.2 %psum.55 = f32[1024]{0:T(1024)S(1)} all-reduce(f32[1024]{0:T(1024)S(1)} %bitcast.20), channel_id=1, replica_groups=mesh['dp'=64,'code'=8] {'dp'}, use_global_device_ids=true, to_apply=%region_10.0 | all-reduce | flops 1024 | bytes 8192 | tf_op jit(solution)/shard_map/psum | solution.py:64
  646.6 0.0 reduce-scatter.5.cloned.1.call-done
  646.6 0.0 copy-done.3
  646.6 1.7 sub.11
  648.3 19.1 %reduce-scatter.3.cloned.1.call-done = f32[1024,8]{0,1:T(8,128)} async-done(((f32[1024,512]{0,1:T(8,128)}), f32[1024,8]{0,1:T(8,128)}) %reduce-scatter.3.cloned.1.call-update) | async-done | bytes 32784 | tf_op jit(solution)/shard_map/reduce_scatter | solution.py:72
  667.4 1.4 broadcast_divide_fusion
  (9 shorter events, 0.1 us)
Async XLA Ops:
  7.2 52.1 %all-gather.2.cloned.1.call-start = ((), (), s32[]{:S(2)}) async-start(), calls=%async_computation.2 | async-start | bytes 2359296 | tf_op jit(solution)/shard_map/all_gather | solution.py:45
  7.9 638.7 %reduce-scatter.5.cloned.1.call-start = ((), (), s32[]{:S(2)}) async-start(), calls=%async_computation.4 | async-start | bytes 2359296 | tf_op jit(solution)/shard_map/reduce_scatter | solution.py:79
  8.6 5.6 copy-start.4
  16.3 1.6 copy-start
  16.3 651.1 %reduce-scatter.3.cloned.1.call-start = ((), (), s32[]{:S(2)}) async-start(), calls=%async_computation.3 | async-start | bytes 2129920 | tf_op jit(solution)/shard_map/reduce_scatter | solution.py:72
  59.2 2.2 copy-start.1
  484.7 22.7 %copy-start.2 = (f32[1024,512]{1,0:T(8,128)S(1)}, f32[1024,512]{1,0:T(8,128)}, u32[]{:S(2)}) copy-start(f32[1024,512]{1,0:T(8,128)} %all-gather.2.cloned.1.call-done) | copy-start | bytes 6291460
  517.8 128.8 %copy-start.3 = (f32[128,512]{1,0:T(8,128)S(1)}, f32[128,512]{1,0:T(8,128)}, u32[]{:S(2)}) copy-start(f32[128,512]{1,0:T(8,128)} %param.3) | copy-start | bytes 786436
Sparse Core Ops, SparseCore 0:
  10.1 49.1 all-gather.1
  62.1 43.7 reduce-scatter.4
  517.9 149.3 reduce-scatter.2
where the time goes:
time: 676 us; the launch traced here: 675 us
  blocking collectives  533 us (79%)
  waiting for transfers between devices  60.9 us (9%)
  matrix products  51.6 us (8%)
  between operations  13.9 us (2%)
  other arithmetic  7.99 us (1%)
  local copies, waits for them, and re-layouts  7.4 us (1%)
    psum x3, blocking collectives, column_scale(): summed = lax.psum(col_part, 'dp')  363 us
    psum x1, blocking collectives, body(): mass = lax.psum(col_part, 'dp')  124 us
    psum x3, blocking collectives, row_scaling(): summed = lax.psum(row_part, 'code')  46.7 us
    all_gather x1, waiting for transfers between devices, body(): gathered = lax.all_gather(items, 'code', axis=0, tiled=True)  41.1 us
    reduce_scatter x1, waiting for transfers between devices, body(): lax.psum_scatter(numerator, 'dp', scatter_dimension=1, tiled=True)  19.1 us
    dot_general x3, matrix products, body(): jnp.dot(kernel_vals, col_scale, precision=lax.Precision.HIGHEST, preferre...  18.7 us
  transfers between devices with their start and end apart: 3, of which 2 were waited for; matrix products, arithmetic and copies ran while one was open for 9% of the time, Pallas kernels for 0%

commit v1 on v0

--- a/solution.py
+++ b/solution.py
@@ -42,7 +42,15 @@
     own_rows = items.shape[0]
     total_items = own_rows * code_count * dp_count
     scaled = unit_rows(codewords) * (inverse_temp / width)
-    gathered = lax.all_gather(items, "code", axis=0, tiled=True)
+    gathered = jnp.concatenate(
+        lax.all_to_all(
+            jnp.stack([items for _ in range(lax.axis_size("code"))], 0),
+            axis_name="code",
+            split_axis=0,
+            concat_axis=0,
+        ),
+        0,
+    )
     kernel_vals = kernel_of(gathered, scaled)
     col_part = jnp.sum(kernel_vals, axis=0)
     row_scale = jnp.ones((kernel_vals.shape[0],), jnp.float32)

time: 676 us -> 703 us (1.040)
  waiting for transfers between devices: 60.9 us -> 71.4 us
  starting transfers between devices: 0.12 us -> 10.5 us
    all_to_all x0 -> x1, waiting for transfers between devices: none -> 52.1 us  [body(): lax.all_to_all(jnp.stack([items for _ in range(lax.axis_size('code'))], 0...]
    all_gather x1 -> x0, waiting for transfers between devices: 41.1 us -> none  [body(): gathered = lax.all_gather(items, 'code', axis=0, tiled=True)]
    all_to_all x0 -> x1, starting transfers between devices: none -> 10.4 us  [body(): lax.all_to_all(jnp.stack([items for _ in range(lax.axis_size('code'))], 0...]
where the time goes in v1:
time: 703 us; the launch traced here: 702 us
  blocking collectives  536 us (76%)
  waiting for transfers between devices  71.4 us (10%)
  matrix products  49.5 us (7%)
  between operations  14.2 us (2%)
  other arithmetic  12.1 us (2%)
  starting transfers between devices  10.5 us (1%)
  local copies, waits for them, and re-layouts  8.35 us (1%)
    psum x3, blocking collectives, column_scale(): summed = lax.psum(col_part, 'dp')  367 us
    psum x1, blocking collectives, body(): mass = lax.psum(col_part, 'dp')  124 us
    all_to_all x1, waiting for transfers between devices, body(): lax.all_to_all(jnp.stack([items for _ in range(lax.axis_size('code'))], 0...  52.1 us
    psum x3, blocking collectives, row_scaling(): summed = lax.psum(row_part, 'code')  44.7 us
    reduce_scatter x1, waiting for transfers between devices, body(): lax.psum_scatter(numerator, 'dp', scatter_dimension=1, tiled=True)  19.3 us
    dot_general x3, matrix products, body(): jnp.dot(kernel_vals, col_scale, precision=lax.Precision.HIGHEST, preferre...  18.5 us
  transfers between devices with their start and end apart: 3, of which 2 were waited for; matrix products, arithmetic and copies ran while one was open for 9% of the time, Pallas kernels for 0%

profile of v1, /device:TPU:16, one launch (start us, length us, event | category | flops | bytes accessed | tf_op | source)
XLA Modules:
  0.0 702.0 jit_solution(9531580389538227329)
XLA Ops:
  7.2 2.6 stack.2
  9.7 0.0 copy-start.3
  9.7 0.0 copy-start.1
  9.7 10.4 %all-to-all-start = ((f32[8,128,512]{2,1,0:T(8,128)}), f32[8,128,512]{2,1,0:T(8,128)}, u32[]{:S(2)}, u32[]{:S(2)}) async-start(f32[8,128,512]{2,1,0:T(8,128)} %stack.2), calls=%async_computation | async-start | bytes 4194304 | tf_op jit(solution)/shard_map/all_to_all | solution.py:46
  20.2 0.0 reduce-scatter.5.cloned.1.call-start
  20.2 0.0 copy-done.3
  20.3 0.0 copy-done.1
  20.3 4.9 gather_fusion
  25.2 3.1 select_select_fusion
  28.3 0.0 reduce-scatter.5.cloned.1.call-update
  28.4 0.0 reduce-scatter.3.cloned.1.call-start
  28.4 0.2 multiply_reduce_fusion
  28.6 52.1 %all-to-all-done = f32[8,128,512]{2,1,0:T(8,128)} async-done(((f32[8,128,512]{2,1,0:T(8,128)}), f32[8,128,512]{2,1,0:T(8,128)}, u32[]{:S(2)}, u32[]{:S(2)}) %all-to-all-start) | async-done | bytes 2097184 | tf_op jit(solution)/shard_map/all_to_all | solution.py:46
  80.7 1.8 multiply_reduce_fusion.1
  82.6 1.8 bitcast_multiply_fusion.1
  84.4 9.1 %exponential_reduce_fusion = (f32[1024]{0:T(1024)S(1)}, f32[1024,1024]{1,0:T(8,128)}) fusion(f32[1024,512]{1,0:T(8,128)S(1)} %bitcast_multiply_fusion.1, f32[1024,512]{1,0:T(8,128)S(1)} %copy-done.1, f32[1024]{0:T(1024)S(1)} %add_rsqrt_fusion), kind=kOutput, calls=%fused_computation.15 | convolution fusion | flops 6444547072 | bytes 8396800 | tf_op jit(solution)/shard_map/dot_general | solution.py:18
  93.5 119.0 %psum.49 = f32[1024]{0:T(1024)S(1)} all-reduce(f32[1024]{0:T(1024)S(1)} %get-tuple-element.4), channel_id=1, replica_groups=mesh['dp'=64,'code'=8] {'dp'}, use_global_device_ids=true, to_apply=%region_3.0 | all-reduce | flops 1024 | bytes 8192 | tf_op jit(solution)/shard_map/psum | solution.py:28
  212.4 6.2 fusion.12
  218.6 14.2 %psum.50 = f32[1024]{0:T(1024)S(1)} all-reduce(f32[1024]{0:T(1024)S(1)} %bitcast.28), channel_id=1, replica_groups=mesh['dp'=64,'code'=8] {'code'}, use_global_device_ids=true, to_apply=%region_4.0 | all-reduce | flops 1024 | bytes 8192 | tf_op jit(solution)/shard_map/psum | solution.py:33
  232.7 4.5 fusion.10
  237.2 124.2 %psum.51 = f32[1024]{0:T(1024)S(1)} all-reduce(f32[1024]{0:T(1024)S(1)} %bitcast.30), channel_id=1, replica_groups=mesh['dp'=64,'code'=8] {'dp'}, use_global_device_ids=true, to_apply=%region_5.0 | all-reduce | flops 1024 | bytes 8192 | tf_op jit(solution)/shard_map/psum | solution.py:28
  361.5 6.2 fusion.8
  367.6 16.2 %psum.52 = f32[1024]{0:T(1024)S(1)} all-reduce(f32[1024]{0:T(1024)S(1)} %bitcast.32), channel_id=1, replica_groups=mesh['dp'=64,'code'=8] {'code'}, use_global_device_ids=true, to_apply=%region_6.0 | all-reduce | flops 1024 | bytes 8192 | tf_op jit(solution)/shard_map/psum | solution.py:33
  383.8 4.5 fusion.6
  388.3 124.0 %psum.53 = f32[1024]{0:T(1024)S(1)} all-reduce(f32[1024]{0:T(1024)S(1)} %bitcast.34), channel_id=1, replica_groups=mesh['dp'=64,'code'=8] {'dp'}, use_global_device_ids=true, to_apply=%region_7.0 | all-reduce | flops 1024 | bytes 8192 | tf_op jit(solution)/shard_map/psum | solution.py:28
  512.3 6.2 fusion.4
  518.5 14.4 %psum.54 = f32[1024]{0:T(1024)S(1)} all-reduce(f32[1024]{0:T(1024)S(1)} %bitcast.36), channel_id=1, replica_groups=mesh['dp'=64,'code'=8] {'code'}, use_global_device_ids=true, to_apply=%region_8.0 | all-reduce | flops 1024 | bytes 8192 | tf_op jit(solution)/shard_map/psum | solution.py:33
  532.9 0.0 copy-start
  532.9 1.9 bitcast_multiply_fusion
  534.8 0.9 copy-done
  535.7 8.4 %fusion.2 = f32[1024,512]{0,1:T(8,128)} fusion(f32[1024,512]{1,0:T(8,128)S(1)} %bitcast_multiply_fusion, f32[1024,1024]{1,0:T(8,128)S(1)} %copy-done), kind=kOutput, calls=%fused_computation.3 | convolution fusion | flops 6442450944 | bytes 8388608 | tf_op jit(solution)/shard_map/dot_general | solution.py:73
  544.1 0.0 reduce-scatter.3.cloned.1.call-update
  544.2 0.0 copy-start.2
  544.2 4.5 fusion
  548.7 124.1 %psum.55 = f32[1024]{0:T(1024)S(1)} all-reduce(f32[1024]{0:T(1024)S(1)} %bitcast.27), channel_id=1, replica_groups=mesh['dp'=64,'code'=8] {'dp'}, use_global_device_ids=true, to_apply=%region_10.0 | all-reduce | flops 1024 | bytes 8192 | tf_op jit(solution)/shard_map/psum | solution.py:72
  672.8 0.0 reduce-scatter.5.cloned.1.call-done
  672.8 0.0 copy-done.2
  672.8 1.7 sub.11
  674.5 19.3 %reduce-scatter.3.cloned.1.call-done = f32[1024,8]{0,1:T(8,128)} async-done(((f32[1024,512]{0,1:T(8,128)}), f32[1024,8]{0,1:T(8,128)}) %reduce-scatter.3.cloned.1.call-update) | async-done | bytes 32784 | tf_op jit(solution)/shard_map/reduce_scatter | solution.py:80
  693.8 1.4 broadcast_divide_fusion
  (10 shorter events, 0.1 us)
Async XLA Ops:
  9.7 10.5 %copy-start.3 = (s32[1024]{0:T(1024)S(1)}, s32[1024]{0:T(1024)}, u32[]{:S(2)}) copy-start(s32[1024]{0:T(1024)} %param.5) | copy-start | bytes 12292
  9.7 10.5 %copy-start.1 = (f32[1024,512]{1,0:T(8,128)S(1)}, f32[1024,512]{1,0:T(8,128)}, u32[]{:S(2)}) copy-start(f32[1024,512]{1,0:T(8,128)} %param.4) | copy-start | bytes 6291460
  9.7 71.0 %all-to-all-start = ((f32[8,128,512]{2,1,0:T(8,128)}), f32[8,128,512]{2,1,0:T(8,128)}, u32[]{:S(2)}, u32[]{:S(2)}) async-start(f32[8,128,512]{2,1,0:T(8,128)} %stack.2), calls=%async_computation | async-start | bytes 4194304 | tf_op jit(solution)/shard_map/all_to_all | solution.py:46
  20.2 652.6 %reduce-scatter.5.cloned.1.call-start = ((), (), s32[]{:S(2)}) async-start(), calls=%async_computation.4 | async-start | bytes 2359296 | tf_op jit(solution)/shard_map/reduce_scatter | solution.py:87
  28.4 665.4 %reduce-scatter.3.cloned.1.call-start = ((), (), s32[]{:S(2)}) async-start(), calls=%async_computation.3 | async-start | bytes 2129920 | tf_op jit(solution)/shard_map/reduce_scatter | solution.py:80
  532.9 2.8 copy-start
  544.2 128.6 %copy-start.2 = (f32[128,512]{1,0:T(8,128)S(1)}, f32[128,512]{1,0:T(8,128)}, u32[]{:S(2)}) copy-start(f32[128,512]{1,0:T(8,128)} %param.3) | copy-start | bytes 786436
Sparse Core Ops, SparseCore 0:
  28.5 63.7 reduce-scatter.4
  544.3 149.4 reduce-scatter.2
